TPU v7x, 32 devices: a whole 2x2x4 slice. The times are simulated.
32 devices in a mesh: seg: 4 (over z), mpo: 4 (over x, core), sec: 2 (over y).
Axes of the slice: x: 2, y: 2, z: 4, core: 2. Of those that a mesh axis runs over, the one named last changes fastest.
Arguments:
- state: bfloat16 [4, 1024, 1024], P('seg', 'sec'), may hold values from -6 to 6
- left_env: bfloat16 [4, 12, 1024, 1024], P('seg', 'mpo', 'sec'), may hold values from -0.1875 to 0.1875
- right_env: bfloat16 [4, 12, 1024, 1024], P('seg', 'mpo'), may hold values from -0.1875 to 0.1875
- inv_singular: float32 [4, 1024], P('seg'), may hold values from 0.5 to 2
- sketch_cols: bfloat16 [4, 2, 1024, 256], P('seg'), may hold values from -6 to 6
- kept_ranks: int32 [4], P('seg'), may hold values from 128 to 256, as said below
Outputs:
- final_state: bfloat16 [4, 1024, 1024], P('seg', 'sec')
Inputs may be any that keep to these rules, and one draw needn't show every extreme that they name: `kept_ranks`: each segment keeps between 128 and 256 ranks; some segment keeps exactly 256.
All inputs are finite; a program needn't handle non-finite values.
Results may differ from a plain program's by a relative error of at most 0.025.
Values may be sent and summed in bfloat16 or wider, within the bound.
No kernel may reach another device: no remote copies, remote signals or barrier semaphores. Data moves between devices by JAX's collectives and lax.ppermute only.
A program may use at most 128 MiB of HBM per device.

v0:
```python
import jax
import jax.numpy as jnp
from jax import lax
from jax.sharding import PartitionSpec as P

ITERS = 2
TAU = 0.3
MOMENTUM = 0.5
EPS = 1e-06


def from_behind(block, axis, distance):
    devices = range(lax.axis_size(axis))
    route = [(i - distance, i) for i in devices if i - distance in devices]
    return lax.ppermute(block, axis, route)


def left_products(left, rows):
    return jnp.einsum(
        "kij,jn->kin",
        left,
        lax.all_gather(rows, "sec", axis=0, tiled=True),
        preferred_element_type=jnp.float32,
    )


def gradient_step(rows, previous, left, right):
    width = rows.shape[1]
    first = left_products(left, rows).astype(jnp.bfloat16)
    partial_sum = jnp.einsum("kij,kjn->in", first, right, preferred_element_type=jnp.float32)
    total = lax.psum(partial_sum, "mpo")
    shifted = rows.astype(jnp.float32) - TAU * total
    if previous is not None:
        shifted = shifted - MOMENTUM * previous.astype(jnp.float32)
    squares = lax.psum(jnp.sum(shifted * shifted), "sec")
    return (shifted * (width * lax.rsqrt(squares + EPS))).astype(jnp.bfloat16)


def run_steps(start_rows, left, right):
    current = start_rows
    previous = None
    for step in range(ITERS):
        current, previous = (gradient_step(current, previous, left, right), current)
    return current


def truncate(rows, omega, rank):
    columns = omega.shape[1]
    sketch = jnp.dot(rows, omega, preferred_element_type=jnp.float32)
    keep = (jnp.arange(columns) < rank).astype(jnp.float32)
    as_float = rows.astype(jnp.float32)
    gram, cross = lax.psum(
        (
            jnp.dot(sketch.T, sketch, precision=lax.Precision.HIGHEST),
            jnp.dot(sketch.T, as_float, precision=lax.Precision.HIGHEST),
        ),
        "sec",
    )
    factor = jnp.linalg.cholesky(gram)
    basis = (
        lax.linalg.triangular_solve(factor, sketch.T, left_side=True, lower=True).T * keep[None, :]
    )
    coeffs = lax.linalg.triangular_solve(factor, cross, left_side=True, lower=True) * keep[:, None]
    return jnp.dot(basis, coeffs, precision=lax.Precision.HIGHEST).astype(jnp.bfloat16)


def on_device(state, left_env, right_env, inv_singular, sketch_cols, kept_ranks):
    rows = state[0]
    left = left_env[0]
    right = right_env[0]
    scales = inv_singular[0]
    rank = kept_ranks[0]
    width = rows.shape[1]
    neighbour = from_behind(rows, "seg", 1)
    merged = (rows.astype(jnp.float32) + neighbour.astype(jnp.float32) * scales[None, :]).astype(
        jnp.bfloat16
    )
    current = run_steps(merged, left, right)
    middle = truncate(current, sketch_cols[0, 0], rank)
    expanded = left_products(left, middle).astype(jnp.bfloat16)
    summed = lax.psum_scatter(
        jnp.einsum("ia,kin->akn", middle, expanded, preferred_element_type=jnp.float32),
        "sec",
        scatter_dimension=0,
        tiled=True,
    )
    message = (summed * (1.0 / width)).astype(jnp.bfloat16)
    arrived = from_behind(message, "seg", 1)
    left_next = (
        left.astype(jnp.float32) + jnp.transpose(arrived.astype(jnp.float32), (1, 0, 2))
    ).astype(jnp.bfloat16)
    neighbour_two = from_behind(middle, "seg", -1)
    merged_two = (
        middle.astype(jnp.float32) + neighbour_two.astype(jnp.float32) * scales[None, :]
    ).astype(jnp.bfloat16)
    current = run_steps(merged_two, left_next, right)
    final_rows = truncate(current, sketch_cols[0, 1], rank)
    return final_rows[None]


def solution(mesh):
    return jax.shard_map(
        on_device,
        mesh=mesh,
        in_specs=(
            P("seg", "sec", None),
            P("seg", "mpo", "sec", None),
            P("seg", "mpo", None, None),
            P("seg", None),
            P("seg", None, None, None),
            P("seg"),
        ),
        out_specs=P("seg", "sec", None),
        check_vma=False,
    )
```

profile of v0, /device:TPU:0, one launch (start us, length us, event | category | flops | bytes accessed | tf_op | source)
XLA Modules:
  0.0 956.5 jit_solution(16439634779600430897)
XLA Ops:
  11.5 22.6 %collective-permute-done = bf16[512,1024]{1,0:T(8,128)(2,1)S(1)} collective-permute-done((bf16[512,1024]{1,0:T(8,128)(2,1)}, bf16[512,1024]{1,0:T(8,128)(2,1)S(1)}, u32[]{:S(2)}, u32[]{:S(2)}) %collective-permute-start) | collective-permute-done | bytes 1048608 | tf_op jit(solution)/shard_map/ppermute | solution.py:15
  36.9 35.3 %all-gather.6.cloned.1.call-done = bf16[1024,1024]{1,0:T(8,128)(2,1)} async-done(((bf16[512,1024]{1,0:T(8,128)(2,1)}), bf16[1024,1024]{1,0:T(8,128)(2,1)}) %all-gather.6.cloned.1.call-update) | async-done | bytes 2097168 | tf_op jit(solution)/shard_map/all_gather | solution.py:22
  77.4 7.5 fusion.33
  85.1 51.5 %all-reduce.10.cloned.1.call-done = f32[512,1024]{1,0:T(8,128)} async-done(((f32[512,1024]{1,0:T(8,128)}), f32[512,1024]{1,0:T(8,128)}) %all-reduce.10.cloned.1.call-update) | async-done | bytes 2097168 | tf_op jit(solution)/shard_map/psum | solution.py:31
  139.4 5.5 psum.85
  147.3 33.1 %all-gather.8.cloned.1.call-done = bf16[1024,1024]{1,0:T(8,128)(2,1)} async-done(((bf16[512,1024]{1,0:T(8,128)(2,1)}), bf16[1024,1024]{1,0:T(8,128)(2,1)}) %all-gather.8.cloned.1.call-update) | async-done | bytes 2097168 | tf_op jit(solution)/shard_map/all_gather | solution.py:22
  180.4 5.9 fusion.15
  186.4 7.5 fusion.38
  194.0 51.5 %all-reduce.12.cloned.1.call-done = f32[512,1024]{1,0:T(8,128)} async-done(((f32[512,1024]{1,0:T(8,128)}), f32[512,1024]{1,0:T(8,128)}) %all-reduce.12.cloned.1.call-update) | async-done | bytes 2097168 | tf_op jit(solution)/shard_map/psum | solution.py:31
  261.9 45.3 %all-reduce.20.cloned.1.call-done = (f32[256,1024]{1,0:T(8,128)}, f32[256,256]{0,1:T(8,128)}) async-done(((f32[256,1024]{1,0:T(8,128)}, f32[256,256]{0,1:T(8,128)}), (f32[256,1024]{1,0:T(8,128)}, f32[256,256]{0,1:T(8,128)})) %all-reduce.20.cloned.1.call-update) | async-done | bytes 1310736 | tf_op jit(solution)/shard_map/psum | solution.py:52
  309.2 11.7 %cholesky.130 = f32[128,128]{1,0:T(8,128)S(1)} custom-call(f32[128,128]{1,0:T(8,128)S(1)} %cholesky.194), custom_call_target="Cholesky" | custom-call | tf_op jit(solution)/shard_map/jit(cholesky)/cholesky | solution.py:59
  321.0 9.8 %custom-call.17 = f32[1,128,128]{1,2,0:T(8,128)S(1)} custom-call(f32[1,128,128]{2,1,0:T(8,128)S(1)} %get-tuple-element.71), custom_call_target="InvertDiagBlocksLowerTriangular" | custom-call | tf_op jit(solution)/shard_map/jit(cholesky)/cholesky | solution.py:59
  331.3 11.7 %cholesky.147 = f32[128,128]{1,0:T(8,128)S(1)} custom-call(f32[128,128]{1,0:T(8,128)S(1)} %convolution_subtract_fusion.5), custom_call_target="Cholesky" | custom-call | tf_op jit(solution)/shard_map/jit(cholesky)/cholesky | solution.py:59
  349.8 19.7 %custom-call.18 = f32[2,128,128]{1,2,0:T(8,128)S(1)} custom-call(f32[2,128,128]{2,1,0:T(8,128)S(1)} %get-tuple-element.36), custom_call_target="InvertDiagBlocksLowerTriangular" | custom-call | tf_op jit(solution)/shard_map/triangular_solve/custom-call.0 | solution.py:61
  375.9 33.2 %all-gather.10.cloned.1.call-done = bf16[1024,1024]{1,0:T(8,128)(2,1)} async-done(((bf16[512,1024]{1,0:T(8,128)(2,1)}), bf16[1024,1024]{1,0:T(8,128)(2,1)}) %all-gather.10.cloned.1.call-update) | async-done | bytes 2097168 | tf_op jit(solution)/shard_map/all_gather | solution.py:22
  409.1 11.1 %fusion.9 = f32[1024,3,1024]{2,0,1:T(8,128)} fusion(bf16[1,3,512,1024]{3,2,1,0:T(8,128)(2,1)S(1)} %copy-done.11, bf16[1024,1024]{1,0:T(8,128)(2,1)} %all-gather.10.cloned.1.call-done, bf16[512,1024]{1,0:T(8,128)(2,1)} %convolution_convert_fusion.1), kind=kOutput, calls=%fused_computation.15 | convolution fusion | flops 6444023808 | bytes 18874368 | tf_op jit(solution)/shard_map/ia,kin->akn/dot_general | solution.py:82
  422.7 142.1 %reduce-scatter.2.cloned.1.call-done = f32[512,3,1024]{2,0,1:T(8,128)} async-done(((f32[1024,3,1024]{2,0,1:T(8,128)}), f32[512,3,1024]{2,0,1:T(8,128)}) %reduce-scatter.2.cloned.1.call-update) | async-done | bytes 6291472 | tf_op jit(solution)/shard_map/reduce_scatter | solution.py:81
  576.9 30.5 %all-gather.12.cloned.1.call-done = bf16[1024,1024]{1,0:T(8,128)(2,1)} async-done(((bf16[512,1024]{1,0:T(8,128)(2,1)}), bf16[1024,1024]{1,0:T(8,128)(2,1)}) %all-gather.12.cloned.1.call-update) | async-done | bytes 2097168 | tf_op jit(solution)/shard_map/all_gather | solution.py:22
  607.4 33.9 %collective-permute-done.2 = bf16[512,3,1024]{2,0,1:T(8,128)(2,1)} collective-permute-done((bf16[512,3,1024]{2,0,1:T(8,128)(2,1)}, bf16[512,3,1024]{2,0,1:T(8,128)(2,1)}, u32[]{:S(2)}, u32[]{:S(2)}) %collective-permute-start.2) | collective-permute-done | bytes 3145760 | tf_op jit(solution)/shard_map/ppermute | solution.py:15
  641.3 6.9 fusion.28
  648.2 7.6 fusion.43
  655.9 52.5 %all-reduce.14.cloned.1.call-done = f32[512,1024]{1,0:T(8,128)} async-done(((f32[512,1024]{1,0:T(8,128)}), f32[512,1024]{1,0:T(8,128)}) %all-reduce.14.cloned.1.call-update) | async-done | bytes 2097168 | tf_op jit(solution)/shard_map/psum | solution.py:31
  718.9 33.3 %all-gather.14.cloned.1.call-done = bf16[1024,1024]{1,0:T(8,128)(2,1)} async-done(((bf16[512,1024]{1,0:T(8,128)(2,1)}), bf16[1024,1024]{1,0:T(8,128)(2,1)}) %all-gather.14.cloned.1.call-update) | async-done | bytes 2097168 | tf_op jit(solution)/shard_map/all_gather | solution.py:22
  752.3 6.9 fusion.26
  759.2 7.5 fusion.48
  766.8 51.5 %all-reduce.16.cloned.1.call-done = f32[512,1024]{1,0:T(8,128)} async-done(((f32[512,1024]{1,0:T(8,128)}), f32[512,1024]{1,0:T(8,128)}) %all-reduce.16.cloned.1.call-update) | async-done | bytes 2097168 | tf_op jit(solution)/shard_map/psum | solution.py:31
  821.0 5.8 psum.93
  834.0 46.2 %all-reduce.18.cloned.1.call-done = (f32[256,1024]{1,0:T(8,128)}, f32[256,256]{0,1:T(8,128)}) async-done(((f32[256,1024]{1,0:T(8,128)}, f32[256,256]{0,1:T(8,128)}), (f32[256,1024]{1,0:T(8,128)}, f32[256,256]{0,1:T(8,128)})) %all-reduce.18.cloned.1.call-update) | async-done | bytes 1310736 | tf_op jit(solution)/shard_map/psum | solution.py:52
  882.2 11.7 %cholesky.164 = f32[128,128]{1,0:T(8,128)S(1)} custom-call(f32[128,128]{1,0:T(8,128)S(1)} %cholesky.197), custom_call_target="Cholesky" | custom-call | tf_op jit(solution)/shard_map/jit(cholesky)/cholesky | solution.py:59
  894.0 9.8 %custom-call.20 = f32[1,128,128]{1,2,0:T(8,128)S(1)} custom-call(f32[1,128,128]{2,1,0:T(8,128)S(1)} %get-tuple-element.67), custom_call_target="InvertDiagBlocksLowerTriangular" | custom-call | tf_op jit(solution)/shard_map/jit(cholesky)/cholesky | solution.py:59
  904.3 11.9 %cholesky.181 = f32[128,128]{1,0:T(8,128)S(1)} custom-call(f32[128,128]{1,0:T(8,128)S(1)} %convolution_subtract_fusion.4), custom_call_target="Cholesky" | custom-call | tf_op jit(solution)/shard_map/jit(cholesky)/cholesky | solution.py:59
  923.2 19.7 %custom-call.21 = f32[2,128,128]{1,2,0:T(8,128)S(1)} custom-call(f32[2,128,128]{2,1,0:T(8,128)S(1)} %get-tuple-element.38), custom_call_target="InvertDiagBlocksLowerTriangular" | custom-call | tf_op jit(solution)/shard_map/triangular_solve/custom-call.0 | solution.py:61
  (130 shorter events, 103.1 us)
Async XLA Ops:
  6.5 65.7 %all-gather.6.cloned.1.call-start = ((), (), s32[]{:S(2)}) async-start(), calls=%async_computation.1 | async-start | bytes 3145728 | tf_op jit(solution)/shard_map/all_gather | solution.py:22
  6.5 27.6 %collective-permute-start = (bf16[512,1024]{1,0:T(8,128)(2,1)}, bf16[512,1024]{1,0:T(8,128)(2,1)S(1)}, u32[]{:S(2)}, u32[]{:S(2)}) collective-permute-start(bf16[512,1024]{1,0:T(8,128)(2,1)} %bitcast.191), channel_id=1, source_target_pairs={{0,8},{8,16},{16,24},{1,9},{9,17},{17,25},{2,10},{10,18},{18,26},{... | collective-permute-start | bytes 3145736 | tf_op jit(solution)/shard_map/ppermute | solution.py:15
  34.2 38.0 %copy-start.10 = (bf16[1,3,512,1024]{3,2,1,0:T(8,128)(2,1)S(1)}, bf16[1,3,512,1024]{3,2,1,0:T(8,128)(2,1)}, u32[]{:S(2)}) copy-start(bf16[1,3,512,1024]{3,2,1,0:T(8,128)(2,1)} %param.12) | copy-start | bytes 9437188
  36.9 99.6 %all-reduce.10.cloned.1.call-start = ((), (), s32[]{:S(2)}) async-start(), calls=%async_computation.2 | async-start | bytes 4194304 | tf_op jit(solution)/shard_map/psum | solution.py:31
  85.0 51.6 %copy-start.1 = (bf16[512,1024]{1,0:T(8,128)(2,1)S(1)}, bf16[512,1024]{1,0:T(8,128)(2,1)}, u32[]{:S(2)}) copy-start(bf16[512,1024]{1,0:T(8,128)(2,1)} %add_convert_fusion.1) | copy-start | bytes 3145732
  85.0 95.4 %all-gather.8.cloned.1.call-start = ((), (), s32[]{:S(2)}) async-start(), calls=%async_computation.3 | async-start | bytes 3145728 | tf_op jit(solution)/shard_map/all_gather | solution.py:22
  136.5 9.1 copy-start.5
  147.1 98.4 %all-reduce.12.cloned.1.call-start = ((), (), s32[]{:S(2)}) async-start(), calls=%async_computation.4 | async-start | bytes 4194304 | tf_op jit(solution)/shard_map/psum | solution.py:31
  193.9 51.6 %copy-start.3 = (bf16[512,1024]{1,0:T(8,128)(2,1)S(1)}, bf16[512,1024]{1,0:T(8,128)(2,1)}, u32[]{:S(2)}) copy-start(bf16[512,1024]{1,0:T(8,128)(2,1)} %multiply_convert_fusion.4) | copy-start | bytes 3145732
  193.9 113.2 %all-reduce.20.cloned.1.call-start = ((), (), s32[]{:S(2)}) async-start(), calls=%async_computation.12 | async-start | bytes 2621440 | tf_op jit(solution)/shard_map/psum | solution.py:52
  254.5 2.3 copy-start.12
  261.0 148.1 %all-gather.10.cloned.1.call-start = ((), (), s32[]{:S(2)}) async-start(), calls=%async_computation.5 | async-start | bytes 3145728 | tf_op jit(solution)/shard_map/all_gather | solution.py:22
  330.8 40.1 %copy-start.7 = (f32[256,1024]{1,0:T(8,128)S(1)}, f32[256,1024]{1,0:T(8,128)}, u32[]{:S(2)}) copy-start(f32[256,1024]{1,0:T(8,128)} %get-tuple-element.58) | copy-start | bytes 3145732
  372.8 36.3 %copy-start.11 = (bf16[1,3,512,1024]{3,2,1,0:T(8,128)(2,1)S(1)}, bf16[1,3,512,1024]{3,2,1,0:T(8,128)(2,1)}, u32[]{:S(2)}) copy-start(bf16[1,3,512,1024]{3,2,1,0:T(8,128)(2,1)} %param.12) | copy-start | bytes 9437188
  375.8 189.0 %reduce-scatter.2.cloned.1.call-start = ((), (), s32[]{:S(2)}) async-start(), calls=%async_computation.6 | async-start | bytes 18874368 | tf_op jit(solution)/shard_map/reduce_scatter | solution.py:81
  420.2 1.2 copy-start.4
  420.2 155.1 %copy-start.9 = (f32[1,1024]{1,0:T(1,128)S(1)}, f32[1,1024]{1,0:T(1,128)}, u32[]{:S(2)}) copy-start(f32[1,1024]{1,0:T(1,128)} %param.14) | copy-start | bytes 12292
  420.2 187.2 %all-gather.12.cloned.1.call-start = ((), (), s32[]{:S(2)}) async-start(), calls=%async_computation.7 | async-start | bytes 3145728 | tf_op jit(solution)/shard_map/all_gather | solution.py:22
  421.4 153.9 %collective-permute-start.1 = (bf16[512,1024]{1,0:T(8,128)(2,1)S(1)}, bf16[512,1024]{1,0:T(8,128)(2,1)S(1)}, u32[]{:S(2)}, u32[]{:S(2)}) collective-permute-start(bf16[512,1024]{1,0:T(8,128)(2,1)S(1)} %copy-done.4), channel_id=1, source_target_pairs={{8,0},{16,8},{24,16},{9,1},{17,9},{25,17},{10,2},{18,10},{26,18},{... | collective-permute-start | bytes 3145736 | tf_op jit(solution)/shard_map/ppermute | solution.py:15
  570.2 71.0 %collective-permute-start.2 = (bf16[512,3,1024]{2,0,1:T(8,128)(2,1)}, bf16[512,3,1024]{2,0,1:T(8,128)(2,1)}, u32[]{:S(2)}, u32[]{:S(2)}) collective-permute-start(bf16[512,3,1024]{2,0,1:T(8,128)(2,1)} %multiply_convert_fusion), channel_id=1, source_target_pairs={{0,8},{8,16},{16,24},{1,9},{9,17},{17,25},{2,10},{10,18},{18,26},{... | collective-permute-start | bytes 9437192 | tf_op jit(solution)/shard_map/ppermute | solution.py:15
  576.7 131.7 %all-reduce.14.cloned.1.call-start = ((), (), s32[]{:S(2)}) async-start(), calls=%async_computation.8 | async-start | bytes 4194304 | tf_op jit(solution)/shard_map/psum | solution.py:31
  655.8 52.6 %copy-start = (bf16[512,1024]{1,0:T(8,128)(2,1)S(1)}, bf16[512,1024]{1,0:T(8,128)(2,1)}, u32[]{:S(2)}) copy-start(bf16[512,1024]{1,0:T(8,128)(2,1)} %add_convert_fusion) | copy-start | bytes 3145732
  655.8 96.4 %all-gather.14.cloned.1.call-start = ((), (), s32[]{:S(2)}) async-start(), calls=%async_computation.9 | async-start | bytes 3145728 | tf_op jit(solution)/shard_map/all_gather | solution.py:22
  708.4 9.1 copy-start.6
  718.9 99.4 %all-reduce.16.cloned.1.call-start = ((), (), s32[]{:S(2)}) async-start(), calls=%async_computation.10 | async-start | bytes 4194304 | tf_op jit(solution)/shard_map/psum | solution.py:31
  766.7 51.6 %copy-start.2 = (bf16[512,1024]{1,0:T(8,128)(2,1)S(1)}, bf16[512,1024]{1,0:T(8,128)(2,1)}, u32[]{:S(2)}) copy-start(bf16[512,1024]{1,0:T(8,128)(2,1)} %multiply_convert_fusion.2) | copy-start | bytes 3145732
  766.7 113.4 %all-reduce.18.cloned.1.call-start = ((), (), s32[]{:S(2)}) async-start(), calls=%async_computation.11 | async-start | bytes 2621440 | tf_op jit(solution)/shard_map/psum | solution.py:52
  827.5 2.3 copy-start.13
  903.8 40.5 %copy-start.8 = (f32[256,1024]{1,0:T(8,128)S(1)}, f32[256,1024]{1,0:T(8,128)}, u32[]{:S(2)}) copy-start(f32[256,1024]{1,0:T(8,128)} %get-tuple-element.56) | copy-start | bytes 3145732
Sparse Core Ops, SparseCore 0:
  37.0 35.1 all-gather.5
  85.1 51.3 all-reduce.9
  147.2 33.1 all-gather.7
  194.0 51.3 all-reduce.11
  261.1 46.0 all-reduce.19
  375.9 33.0 all-gather.9
  420.3 144.4 reduce-scatter.1
  576.8 30.5 all-gather.11
  655.9 52.3 all-reduce.13
  719.0 33.1 all-gather.13
  766.8 51.3 all-reduce.15
  834.1 46.0 all-reduce.17
where the time goes:
time: 962 us; the launch traced here: 956 us
  waiting for transfers between devices  663 us (69%)
  other arithmetic  138 us (14%)
  matrix products  88.1 us (9%)
  blocking collectives  22.4 us (2%)
  between operations  20.6 us (2%)
  starting transfers between devices  12.3 us (1%)
  local copies, waits for them, and re-layouts  11.6 us (1%)
    psum x4, waiting for transfers between devices, gradient_step(): total = lax.psum(partial_sum, 'mpo')  207 us
    all_gather x5, waiting for transfers between devices, left_products(): lax.all_gather(rows, 'sec', axis=0, tiled=True)  165 us
    reduce_scatter x1, waiting for transfers between devices, on_device(): lax.psum_scatter(jnp.einsum('ia,kin->akn', middle, expanded, preferred_el...  142 us
    psum x2, waiting for transfers between devices, truncate(): lax.psum((jnp.dot(sketch.T, sketch, precision=lax.Precision.HIGHEST), jnp...  91.4 us
    another operation x13, other arithmetic, truncate(): factor = jnp.linalg.cholesky(gram)  68.9 us
    ppermute x3, waiting for transfers between devices, from_behind(): return lax.ppermute(block, axis, route)  56.5 us
    another operation x5, other arithmetic, truncate(): lax.linalg.triangular_solve(factor, sketch.T, left_side=True, lower=True)  39.4 us
    dot_general x4, matrix products, gradient_step(): jnp.einsum('kij,kjn->in', first, right, preferred_element_type=jnp.float32)  30.2 us
  transfers between devices with their start and end apart: 15, of which 14 were waited for; matrix products, arithmetic and copies ran while one was open for 1% of the time, Pallas kernels for 0%

commit v1 on v0

--- a/solution.py
+++ b/solution.py
@@ -16,12 +16,26 @@
 
 
 def left_products(left, rows):
-    return jnp.einsum(
-        "kij,jn->kin",
-        left,
-        lax.all_gather(rows, "sec", axis=0, tiled=True),
-        preferred_element_type=jnp.float32,
-    )
+
+    def _turn_joints(chunk):
+        y, x_now, latest = (jax.lax.axis_size("sec"), jax.lax.axis_index("sec"), chunk.shape[0])
+        outcome_arr, state_next = (chunk, 1)
+        while state_next < y:
+            outcome_arr = jnp.concatenate(
+                [
+                    outcome_arr,
+                    jax.lax.ppermute(
+                        outcome_arr,
+                        "sec",
+                        [(hop_no, (hop_no - state_next) % y) for hop_no in range(y)],
+                    ),
+                ],
+                0,
+            )
+            state_next = 2 * state_next
+        return jnp.roll(outcome_arr, x_now * latest, 0)
+
+    return jnp.einsum("kij,jn->kin", left, _turn_joints(rows), preferred_element_type=jnp.float32)
 
 
 def gradient_step(rows, previous, left, right):

time: 962 us -> 920 us (0.956)
  waiting for transfers between devices: 663 us -> 623 us
    all_gather x5 -> x0, waiting for transfers between devices: 165 us -> none  [left_products(): lax.all_gather(rows, 'sec', axis=0, tiled=True)]
    ppermute x0 -> x5, waiting for transfers between devices: none -> 115 us  [_turn_joints(): jax.lax.ppermute(outcome_arr, 'sec', [(hop_no, (hop_no - state_next) % y)...]
    dot_general x4, matrix products: 30.2 us -> 51.7 us  [gradient_step(): jnp.einsum('kij,kjn->in', first, right, preferred_element_type=jnp.float32)]
    dot_general x4 -> x1, matrix products: 24.9 us -> 4.88 us  [left_products(): jnp.einsum('kij,jn->kin', left, _turn_joints(rows), preferred_element_typ...]
  transfers between devices with their start and end apart: 15 -> 15, of which waited for: 14 -> 15; matrix products, arithmetic and copies ran while one was open for 1% -> 0% of each run, Pallas kernels for 0% -> 0%
where the time goes in v1:
time: 920 us; the launch traced here: 914 us
  waiting for transfers between devices  623 us (68%)
  other arithmetic  135 us (15%)
  matrix products  83.9 us (9%)
  blocking collectives  22.6 us (2%)
  between operations  20.4 us (2%)
  starting transfers between devices  17.7 us (2%)
  local copies, waits for them, and re-layouts  10.6 us (1%)
    psum x4, waiting for transfers between devices, gradient_step(): total = lax.psum(partial_sum, 'mpo')  210 us
    reduce_scatter x1, waiting for transfers between devices, on_device(): lax.psum_scatter(jnp.einsum('ia,kin->akn', middle, expanded, preferred_el...  144 us
    ppermute x5, waiting for transfers between devices, _turn_joints(): jax.lax.ppermute(outcome_arr, 'sec', [(hop_no, (hop_no - state_next) % y)...  115 us
    psum x2, waiting for transfers between devices, truncate(): lax.psum((jnp.dot(sketch.T, sketch, precision=lax.Precision.HIGHEST), jnp...  91.4 us
    another operation x13, other arithmetic, truncate(): factor = jnp.linalg.cholesky(gram)  68.9 us
    ppermute x3, waiting for transfers between devices, from_behind(): return lax.ppermute(block, axis, route)  62.8 us
    dot_general x4, matrix products, gradient_step(): jnp.einsum('kij,kjn->in', first, right, preferred_element_type=jnp.float32)  51.7 us
    another operation x5, other arithmetic, truncate(): lax.linalg.triangular_solve(factor, sketch.T, left_side=True, lower=True)  39.4 us
  transfers between devices with their start and end apart: 15, of which 15 were waited for; matrix products, arithmetic and copies ran while one was open for 0% of the time, Pallas kernels for 0%

profile of v1, /device:TPU:0, one launch (start us, length us, event | category | flops | bytes accessed | tf_op | source)
XLA Modules:
  0.0 914.0 jit_solution(1305911314158565149)
XLA Ops:
  11.5 22.6 %collective-permute-done = bf16[512,1024]{1,0:T(8,128)(2,1)S(1)} collective-permute-done((bf16[512,1024]{1,0:T(8,128)(2,1)}, bf16[512,1024]{1,0:T(8,128)(2,1)S(1)}, u32[]{:S(2)}, u32[]{:S(2)}) %collective-permute-start) | collective-permute-done | bytes 1048608 | tf_op jit(solution)/shard_map/ppermute | solution.py:15
  37.3 22.5 %collective-permute-done.1 = bf16[512,1024]{1,0:T(8,128)(2,1)S(1)} collective-permute-done((bf16[512,1024]{1,0:T(8,128)(2,1)S(1)}, bf16[512,1024]{1,0:T(8,128)(2,1)S(1)}, u32[]{:S(2)}, u32[]{:S(2)}) %collective-permute-start.1) | collective-permute-done | bytes 1048608 | tf_op jit(solution)/shard_map/ppermute | solution.py:27
  59.8 12.3 %fusion.82 = f32[512,1024]{1,0:T(8,128)} fusion(bf16[1,3,1024,1024]{3,2,1,0:T(8,128)(2,1)} %param.15, bf16[1,3,512,1024]{3,2,1,0:T(8,128)(2,1)} %param.14, s32[]{:T(128)S(6)} %select_n.23, bf16[512,1024]{1,0:T(8,128)(2,1)S(1)} %add_convert_fusion.1, bf16[512,1024]{1,0:T(8,128)(2,1)S(1)} %collective-permute-done.1), kind=kOutput, calls=%fused_computation.88 | convolution fusion | flops 6452412416 | bytes 13631492 | tf_op jit(solution)/shard_map/kij,kjn->in/dot_general | solution.py:44
  72.3 53.5 %all-reduce.10.cloned.1.call-done = f32[512,1024]{1,0:T(8,128)} async-done(((f32[512,1024]{1,0:T(8,128)}), f32[512,1024]{1,0:T(8,128)}) %all-reduce.10.cloned.1.call-update) | async-done | bytes 2097168 | tf_op jit(solution)/shard_map/psum | solution.py:45
  128.5 5.7 psum.85
  138.5 22.2 %collective-permute-done.2 = bf16[512,1024]{1,0:T(8,128)(2,1)S(1)} collective-permute-done((bf16[512,1024]{1,0:T(8,128)(2,1)S(1)}, bf16[512,1024]{1,0:T(8,128)(2,1)S(1)}, u32[]{:S(2)}, u32[]{:S(2)}) %collective-permute-start.2) | collective-permute-done | bytes 1048608 | tf_op jit(solution)/shard_map/ppermute | solution.py:27
  160.7 12.3 %fusion.91 = f32[512,1024]{1,0:T(8,128)} fusion(bf16[1,3,1024,1024]{3,2,1,0:T(8,128)(2,1)} %param.15, bf16[1,3,512,1024]{3,2,1,0:T(8,128)(2,1)} %param.14, s32[]{:T(128)S(6)} %select_n.23, bf16[512,1024]{1,0:T(8,128)(2,1)S(1)} %multiply_convert_fusion.4, bf16[512,1024]{1,0:T(8,128)(2,1)S(1)} %collective-permute-done.2), kind=kOutput, calls=%fused_computation.89 | convolution fusion | flops 6452412416 | bytes 13631492 | tf_op jit(solution)/shard_map/kij,kjn->in/dot_general | solution.py:44
  173.1 51.7 %all-reduce.12.cloned.1.call-done = f32[512,1024]{1,0:T(8,128)} async-done(((f32[512,1024]{1,0:T(8,128)}), f32[512,1024]{1,0:T(8,128)}) %all-reduce.12.cloned.1.call-update) | async-done | bytes 2097168 | tf_op jit(solution)/shard_map/psum | solution.py:45
  227.6 5.5 psum.87
  241.1 45.2 %all-reduce.20.cloned.1.call-done = (f32[256,1024]{1,0:T(8,128)}, f32[256,256]{0,1:T(8,128)}) async-done(((f32[256,1024]{1,0:T(8,128)}, f32[256,256]{0,1:T(8,128)}), (f32[256,1024]{1,0:T(8,128)}, f32[256,256]{0,1:T(8,128)})) %all-reduce.20.cloned.1.call-update) | async-done | bytes 1310736 | tf_op jit(solution)/shard_map/psum | solution.py:66
  288.6 11.7 %cholesky.130 = f32[128,128]{1,0:T(8,128)S(1)} custom-call(f32[128,128]{1,0:T(8,128)S(1)} %cholesky.194), custom_call_target="Cholesky" | custom-call | tf_op jit(solution)/shard_map/jit(cholesky)/cholesky | solution.py:73
  300.3 9.8 %custom-call.17 = f32[1,128,128]{1,2,0:T(8,128)S(1)} custom-call(f32[1,128,128]{2,1,0:T(8,128)S(1)} %get-tuple-element.72), custom_call_target="InvertDiagBlocksLowerTriangular" | custom-call | tf_op jit(solution)/shard_map/jit(cholesky)/cholesky | solution.py:73
  310.6 11.7 %cholesky.147 = f32[128,128]{1,0:T(8,128)S(1)} custom-call(f32[128,128]{1,0:T(8,128)S(1)} %convolution_subtract_fusion.5), custom_call_target="Cholesky" | custom-call | tf_op jit(solution)/shard_map/jit(cholesky)/cholesky | solution.py:73
  329.1 19.7 %custom-call.18 = f32[2,128,128]{1,2,0:T(8,128)S(1)} custom-call(f32[2,128,128]{2,1,0:T(8,128)S(1)} %get-tuple-element.37), custom_call_target="InvertDiagBlocksLowerTriangular" | custom-call | tf_op jit(solution)/shard_map/triangular_solve/custom-call.0 | solution.py:75
  354.6 24.6 %collective-permute-done.4 = bf16[512,1024]{1,0:T(8,128)(2,1)S(1)} collective-permute-done((bf16[512,1024]{1,0:T(8,128)(2,1)S(1)}, bf16[512,1024]{1,0:T(8,128)(2,1)S(1)}, u32[]{:S(2)}, u32[]{:S(2)}) %collective-permute-start.4) | collective-permute-done | bytes 1048608 | tf_op jit(solution)/shard_map/ppermute | solution.py:27
  384.0 6.4 fusion.9
  390.7 144.4 %reduce-scatter.2.cloned.1.call-done = f32[512,3,1024]{2,0,1:T(8,128)} async-done(((f32[1024,3,1024]{2,0,1:T(8,128)}), f32[512,3,1024]{2,0,1:T(8,128)}) %reduce-scatter.2.cloned.1.call-update) | async-done | bytes 6291472 | tf_op jit(solution)/shard_map/reduce_scatter | solution.py:95
  545.2 25.2 %collective-permute-done.3 = bf16[512,1024]{1,0:T(8,128)(2,1)S(1)} collective-permute-done((bf16[512,1024]{1,0:T(8,128)(2,1)S(1)}, bf16[512,1024]{1,0:T(8,128)(2,1)S(1)}, u32[]{:S(2)}, u32[]{:S(2)}) %collective-permute-start.3) | collective-permute-done | bytes 1048608 | tf_op jit(solution)/shard_map/ppermute | solution.py:15
  571.4 23.1 %collective-permute-done.6 = bf16[512,1024]{1,0:T(8,128)(2,1)S(1)} collective-permute-done((bf16[512,1024]{1,0:T(8,128)(2,1)S(1)}, bf16[512,1024]{1,0:T(8,128)(2,1)S(1)}, u32[]{:S(2)}, u32[]{:S(2)}) %collective-permute-start.6) | collective-permute-done | bytes 1048608 | tf_op jit(solution)/shard_map/ppermute | solution.py:27
  594.6 15.0 %collective-permute-done.5 = bf16[512,3,1024]{2,0,1:T(8,128)(2,1)} collective-permute-done((bf16[512,3,1024]{2,0,1:T(8,128)(2,1)S(1)}, bf16[512,3,1024]{2,0,1:T(8,128)(2,1)}, u32[]{:S(2)}, u32[]{:S(2)}) %collective-permute-start.5) | collective-permute-done | bytes 3145760 | tf_op jit(solution)/shard_map/ppermute | solution.py:15
  609.6 13.6 %fusion.100 = f32[512,1024]{1,0:T(8,128)} fusion(bf16[1,3,1024,1024]{3,2,1,0:T(8,128)(2,1)} %param.15, s32[]{:T(128)S(6)} %select_n.23, bf16[512,1024]{1,0:T(8,128)(2,1)S(1)} %add_convert_fusion, bf16[512,1024]{1,0:T(8,128)(2,1)S(1)} %collective-permute-done.6, bf16[512,3,1024]{2,0,1:T(8,128)(2,1)} %collective-permute-done.5, ...), kind=kOutput, calls=%fused_computation.90 | convolution fusion | flops 6458703872 | bytes 16777220 | tf_op jit(solution)/shard_map/kij,kjn->in/dot_general | solution.py:44
  623.2 52.6 %all-reduce.14.cloned.1.call-done = f32[512,1024]{1,0:T(8,128)} async-done(((f32[512,1024]{1,0:T(8,128)}), f32[512,1024]{1,0:T(8,128)}) %all-reduce.14.cloned.1.call-update) | async-done | bytes 2097168 | tf_op jit(solution)/shard_map/psum | solution.py:45
  678.6 5.5 psum.91
  688.3 22.3 %collective-permute-done.7 = bf16[512,1024]{1,0:T(8,128)(2,1)} collective-permute-done((bf16[512,1024]{1,0:T(8,128)(2,1)S(1)}, bf16[512,1024]{1,0:T(8,128)(2,1)}, u32[]{:S(2)}, u32[]{:S(2)}) %collective-permute-start.7) | collective-permute-done | bytes 1048608 | tf_op jit(solution)/shard_map/ppermute | solution.py:27
  710.6 13.4 %fusion.107 = f32[512,1024]{1,0:T(8,128)} fusion(bf16[1,3,1024,1024]{3,2,1,0:T(8,128)(2,1)} %param.15, s32[]{:T(128)S(6)} %select_n.23, bf16[512,1024]{1,0:T(8,128)(2,1)S(1)} %multiply_convert_fusion.2, bf16[512,1024]{1,0:T(8,128)(2,1)} %collective-permute-done.7, bf16[512,3,1024]{2,0,1:T(8,128)(2,1)} %collective-permute-done.5, ...), kind=kOutput, calls=%fused_computation.91 | convolution fusion | flops 6458703872 | bytes 16777220 | tf_op jit(solution)/shard_map/kij,kjn->in/dot_general | solution.py:44
  724.1 51.7 %all-reduce.16.cloned.1.call-done = f32[512,1024]{1,0:T(8,128)} async-done(((f32[512,1024]{1,0:T(8,128)}), f32[512,1024]{1,0:T(8,128)}) %all-reduce.16.cloned.1.call-update) | async-done | bytes 2097168 | tf_op jit(solution)/shard_map/psum | solution.py:45
  778.6 5.8 psum.93
  791.5 46.2 %all-reduce.18.cloned.1.call-done = (f32[256,1024]{1,0:T(8,128)}, f32[256,256]{0,1:T(8,128)}) async-done(((f32[256,1024]{1,0:T(8,128)}, f32[256,256]{0,1:T(8,128)}), (f32[256,1024]{1,0:T(8,128)}, f32[256,256]{0,1:T(8,128)})) %all-reduce.18.cloned.1.call-update) | async-done | bytes 1310736 | tf_op jit(solution)/shard_map/psum | solution.py:66
  839.8 11.7 %cholesky.164 = f32[128,128]{1,0:T(8,128)S(1)} custom-call(f32[128,128]{1,0:T(8,128)S(1)} %cholesky.197), custom_call_target="Cholesky" | custom-call | tf_op jit(solution)/shard_map/jit(cholesky)/cholesky | solution.py:73
  851.6 9.8 %custom-call.20 = f32[1,128,128]{1,2,0:T(8,128)S(1)} custom-call(f32[1,128,128]{2,1,0:T(8,128)S(1)} %get-tuple-element.68), custom_call_target="InvertDiagBlocksLowerTriangular" | custom-call | tf_op jit(solution)/shard_map/jit(cholesky)/cholesky | solution.py:73
  861.9 12.0 %cholesky.181 = f32[128,128]{1,0:T(8,128)S(1)} custom-call(f32[128,128]{1,0:T(8,128)S(1)} %convolution_subtract_fusion.4), custom_call_target="Cholesky" | custom-call | tf_op jit(solution)/shard_map/jit(cholesky)/cholesky | solution.py:73
  880.7 19.7 %custom-call.21 = f32[2,128,128]{1,2,0:T(8,128)S(1)} custom-call(f32[2,128,128]{2,1,0:T(8,128)S(1)} %get-tuple-element.39), custom_call_target="InvertDiagBlocksLowerTriangular" | custom-call | tf_op jit(solution)/shard_map/triangular_solve/custom-call.0 | solution.py:75
  (104 shorter events, 92.0 us)
Async XLA Ops:
  6.5 119.3 %all-reduce.10.cloned.1.call-start = ((), (), s32[]{:S(2)}) async-start(), calls=%async_computation.1 | async-start | bytes 4194304 | tf_op jit(solution)/shard_map/psum | solution.py:45
  6.5 27.6 %collective-permute-start = (bf16[512,1024]{1,0:T(8,128)(2,1)}, bf16[512,1024]{1,0:T(8,128)(2,1)S(1)}, u32[]{:S(2)}, u32[]{:S(2)}) collective-permute-start(bf16[512,1024]{1,0:T(8,128)(2,1)} %bitcast.221), channel_id=1, source_target_pairs={{0,8},{8,16},{16,24},{1,9},{9,17},{17,25},{2,10},{10,18},{18,26},{... | collective-permute-start | bytes 3145736 | tf_op jit(solution)/shard_map/ppermute | solution.py:15
  35.8 24.1 %collective-permute-start.1 = (bf16[512,1024]{1,0:T(8,128)(2,1)S(1)}, bf16[512,1024]{1,0:T(8,128)(2,1)S(1)}, u32[]{:S(2)}, u32[]{:S(2)}) collective-permute-start(bf16[512,1024]{1,0:T(8,128)(2,1)S(1)} %add_convert_fusion.1), channel_id=1, source_target_pairs={{0,1},{1,0},{2,3},{3,2},{4,5},{5,4},{6,7},{7,6},{8,9},{9,8},{10,11... | collective-permute-start | bytes 3145736 | tf_op jit(solution)/shard_map/ppermute | solution.py:27
  72.2 152.6 %all-reduce.12.cloned.1.call-start = ((), (), s32[]{:S(2)}) async-start(), calls=%async_computation.2 | async-start | bytes 4194304 | tf_op jit(solution)/shard_map/psum | solution.py:45
  136.9 23.7 %collective-permute-start.2 = (bf16[512,1024]{1,0:T(8,128)(2,1)S(1)}, bf16[512,1024]{1,0:T(8,128)(2,1)S(1)}, u32[]{:S(2)}, u32[]{:S(2)}) collective-permute-start(bf16[512,1024]{1,0:T(8,128)(2,1)S(1)} %multiply_convert_fusion.4), channel_id=1, source_target_pairs={{0,1},{1,0},{2,3},{3,2},{4,5},{5,4},{6,7},{7,6},{8,9},{9,8},{10,11... | collective-permute-start | bytes 3145736 | tf_op jit(solution)/shard_map/ppermute | solution.py:27
  173.0 113.3 %all-reduce.20.cloned.1.call-start = ((), (), s32[]{:S(2)}) async-start(), calls=%async_computation.7 | async-start | bytes 2621440 | tf_op jit(solution)/shard_map/psum | solution.py:66
  227.6 8.4 copy-start.4
  240.2 295.0 %reduce-scatter.2.cloned.1.call-start = ((), (), s32[]{:S(2)}) async-start(), calls=%async_computation.3 | async-start | bytes 18874368 | tf_op jit(solution)/shard_map/reduce_scatter | solution.py:95
  286.4 63.9 %copy-start = (f32[256,1024]{1,0:T(8,128)S(1)}, f32[256,1024]{1,0:T(8,128)}, u32[]{:S(2)}) copy-start(f32[256,1024]{1,0:T(8,128)} %get-tuple-element.59) | copy-start | bytes 3145732
  350.3 28.9 %copy-start.3 = (bf16[1,3,512,1024]{3,2,1,0:T(8,128)(2,1)S(1)}, bf16[1,3,512,1024]{3,2,1,0:T(8,128)(2,1)}, u32[]{:S(2)}) copy-start(bf16[1,3,512,1024]{3,2,1,0:T(8,128)(2,1)} %param.14) | copy-start | bytes 9437188
  354.2 25.0 %collective-permute-start.4 = (bf16[512,1024]{1,0:T(8,128)(2,1)S(1)}, bf16[512,1024]{1,0:T(8,128)(2,1)S(1)}, u32[]{:S(2)}, u32[]{:S(2)}) collective-permute-start(bf16[512,1024]{1,0:T(8,128)(2,1)S(1)} %convolution_convert_fusion.1), channel_id=1, source_target_pairs={{0,1},{1,0},{2,3},{3,2},{4,5},{5,4},{6,7},{7,6},{8,9},{9,8},{10,11... | collective-permute-start | bytes 3145736 | tf_op jit(solution)/shard_map/ppermute | solution.py:27
  390.5 179.9 %copy-start.2 = (f32[1,1024]{1,0:T(1,128)S(1)}, f32[1,1024]{1,0:T(1,128)}, u32[]{:S(2)}) copy-start(f32[1,1024]{1,0:T(1,128)} %param.16) | copy-start | bytes 12292
  390.5 285.3 %all-reduce.14.cloned.1.call-start = ((), (), s32[]{:S(2)}) async-start(), calls=%async_computation.4 | async-start | bytes 4194304 | tf_op jit(solution)/shard_map/psum | solution.py:45
  538.8 70.7 %collective-permute-start.5 = (bf16[512,3,1024]{2,0,1:T(8,128)(2,1)S(1)}, bf16[512,3,1024]{2,0,1:T(8,128)(2,1)}, u32[]{:S(2)}, u32[]{:S(2)}) collective-permute-start(bf16[512,3,1024]{2,0,1:T(8,128)(2,1)S(1)} %multiply_convert_fusion), channel_id=1, source_target_pairs={{0,8},{8,16},{16,24},{1,9},{9,17},{17,25},{2,10},{10,18},{18,26},{... | collective-permute-start | bytes 9437192 | tf_op jit(solution)/shard_map/ppermute | solution.py:15
  543.9 26.5 %collective-permute-start.3 = (bf16[512,1024]{1,0:T(8,128)(2,1)S(1)}, bf16[512,1024]{1,0:T(8,128)(2,1)S(1)}, u32[]{:S(2)}, u32[]{:S(2)}) collective-permute-start(bf16[512,1024]{1,0:T(8,128)(2,1)S(1)} %convolution_convert_fusion.1), channel_id=1, source_target_pairs={{8,0},{16,8},{24,16},{9,1},{17,9},{25,17},{10,2},{18,10},{26,18},{... | collective-permute-start | bytes 3145736 | tf_op jit(solution)/shard_map/ppermute | solution.py:15
  570.8 23.7 %collective-permute-start.6 = (bf16[512,1024]{1,0:T(8,128)(2,1)S(1)}, bf16[512,1024]{1,0:T(8,128)(2,1)S(1)}, u32[]{:S(2)}, u32[]{:S(2)}) collective-permute-start(bf16[512,1024]{1,0:T(8,128)(2,1)S(1)} %add_convert_fusion), channel_id=1, source_target_pairs={{0,1},{1,0},{2,3},{3,2},{4,5},{5,4},{6,7},{7,6},{8,9},{9,8},{10,11... | collective-permute-start | bytes 3145736 | tf_op jit(solution)/shard_map/ppermute | solution.py:27
  623.2 152.7 %all-reduce.16.cloned.1.call-start = ((), (), s32[]{:S(2)}) async-start(), calls=%async_computation.5 | async-start | bytes 4194304 | tf_op jit(solution)/shard_map/psum | solution.py:45
  686.8 23.8 %collective-permute-start.7 = (bf16[512,1024]{1,0:T(8,128)(2,1)S(1)}, bf16[512,1024]{1,0:T(8,128)(2,1)}, u32[]{:S(2)}, u32[]{:S(2)}) collective-permute-start(bf16[512,1024]{1,0:T(8,128)(2,1)S(1)} %multiply_convert_fusion.2), channel_id=1, source_target_pairs={{0,1},{1,0},{2,3},{3,2},{4,5},{5,4},{6,7},{7,6},{8,9},{9,8},{10,11... | collective-permute-start | bytes 3145736 | tf_op jit(solution)/shard_map/ppermute | solution.py:27
  724.1 113.5 %all-reduce.18.cloned.1.call-start = ((), (), s32[]{:S(2)}) async-start(), calls=%async_computation.6 | async-start | bytes 2621440 | tf_op jit(solution)/shard_map/psum | solution.py:66
  837.6 64.2 %copy-start.1 = (f32[256,1024]{1,0:T(8,128)S(1)}, f32[256,1024]{1,0:T(8,128)}, u32[]{:S(2)}) copy-start(f32[256,1024]{1,0:T(8,128)} %get-tuple-element.57) | copy-start | bytes 3145732
Sparse Core Ops, SparseCore 0:
  72.3 53.4 all-reduce.9
  173.2 51.5 all-reduce.11
  240.3 46.0 all-reduce.19
  390.6 144.4 reduce-scatter.1
  623.3 52.4 all-reduce.13
  724.2 51.5 all-reduce.15
  791.6 46.0 all-reduce.17
